TPU v7x, 768 devices: a whole 4x8x12 slice. The times are simulated.
768 devices in a mesh: depth: 8 (over y), plane: 96 (over x, z, core).
Axes of the slice: x: 4, y: 8, z: 12, core: 2. Of those that a mesh axis runs over, the one named last changes fastest.
Arguments:
- density: bfloat16 [128, 768, 1536], P('depth', 'plane'), may hold values from -6 to 6
- material: int32 [128, 768, 1536], P('depth', 'plane'), may hold values from 0 to 15
- tf_color: float32 [3, 16], replicated, may hold values from 0.2 to 1
- tf_extinction: float32 [16], replicated, may hold values from 0.5 to 8
Outputs:
- image: float32 [4, 768, 1536], P(None, 'plane', 'depth')
All inputs are finite; a program needn't handle non-finite values.
Results may differ from a plain program's by a relative error of at most 0.0003.
Values may be sent and summed in bfloat16 or wider, within the bound.
A program may use at most 32 MiB of HBM per device.

v0:
```python
import jax
import jax.numpy as jnp
from jax import lax
from jax.sharding import PartitionSpec as P

LEVELS = 16


light_z = 0.64
light_x = 0.48
light_y = 0.6


def with_halo(x, sides, width):
    for axis, dim in sides:
        peers, length = (lax.axis_size(axis), x.shape[dim])
        up = [(i, (i + 1) % peers) for i in range(peers - 1)]
        down = [(j, i) for i, j in up]
        last = lax.slice_in_dim(x, length - width, length, axis=dim)
        initial = lax.slice_in_dim(x, 0, width, axis=dim)
        before = lax.ppermute(last, axis, up)
        after = lax.ppermute(initial, axis, down)
        x = jnp.concatenate([before, x, after], axis=dim)
    return x


def tent_valid(field, axis):
    count = field.shape[axis]
    left = lax.slice_in_dim(field, 0, count - 2, axis=axis)
    middle = lax.slice_in_dim(field, 1, count - 1, axis=axis)
    right = lax.slice_in_dim(field, 2, count, axis=axis)
    return (left + 2.0 * middle + right) * 0.25


def slope_valid(field, axis):
    count = field.shape[axis]
    left = lax.slice_in_dim(field, 0, count - 2, axis=axis)
    right = lax.slice_in_dim(field, 2, count, axis=axis)
    return (right - left) * 0.5


def pad_last(field):
    return jnp.pad(field, ((0, 0), (0, 0), (1, 1)))


def smooth_valid(field):
    return tent_valid(pad_last(tent_valid(tent_valid(field, 0), 1)), 2)


def render_brick(smooth_ext, labels, tf_color, tf_extinction, scale):
    smooth = smooth_ext[1:-1, 1:-1]
    grad_z = slope_valid(tent_valid(pad_last(tent_valid(smooth_ext, 1)), 2), 0)
    grad_x = slope_valid(tent_valid(pad_last(tent_valid(smooth_ext, 0)), 2), 1)
    grad_y = slope_valid(pad_last(tent_valid(tent_valid(smooth_ext, 0), 1)), 2)
    lit = 0.35 + 0.65 * jnp.abs(light_z * grad_z + light_x * grad_x + light_y * grad_y) / jnp.sqrt(
        grad_z * grad_z + grad_x * grad_x + grad_y * grad_y + 1.0
    )
    zeros = jnp.zeros(labels.shape, jnp.float32)
    extinct = zeros
    reds, greens, blues = (zeros, zeros, zeros)
    for level in range(LEVELS):
        match = labels == level
        extinct = jnp.where(match, tf_extinction[level], extinct)
        reds = jnp.where(match, tf_color[0, level], reds)
        greens = jnp.where(match, tf_color[1, level], greens)
        blues = jnp.where(match, tf_color[2, level], blues)
    optical = extinct * (smooth * smooth + 0.25) * scale
    running = jnp.cumsum(optical, axis=0)
    weight = jnp.exp(-(running - optical)) * (1.0 - jnp.exp(-optical)) * lit
    alpha = 1.0 - jnp.exp(-running[-1])
    return jnp.stack(
        [
            jnp.sum(weight * reds, axis=0),
            jnp.sum(weight * greens, axis=0),
            jnp.sum(weight * blues, axis=0),
            alpha,
        ],
        axis=0,
    )


def over_blend(front, back):
    return front + (1.0 - front[3:4]) * back


def shards(density, material, tf_color, tf_extinction):
    bricks = lax.axis_size("depth")
    depth_cells, row_cells, col_cells = density.shape
    total_z = depth_cells * bricks
    total_x = row_cells * lax.axis_size("plane")
    scale = 2.0 / total_z
    padded = with_halo(density, (("depth", 0), ("plane", 1)), 2)
    smooth_ext = smooth_valid(padded.astype(jnp.float32))
    zpos = lax.axis_index("depth") * depth_cells + jnp.arange(depth_cells + 2, dtype=jnp.int32) - 1
    xpos = lax.axis_index("plane") * row_cells + jnp.arange(row_cells + 2, dtype=jnp.int32) - 1
    inside = ((zpos >= 0) & (zpos < total_z))[:, None, None] & ((xpos >= 0) & (xpos < total_x))[
        None, :, None
    ]
    smooth_ext = jnp.where(inside, smooth_ext, jnp.float32(0.0))
    partial_image = render_brick(smooth_ext, material, tf_color, tf_extinction, scale)
    received = lax.all_to_all(partial_image, "depth", split_axis=2, concat_axis=0, tiled=True)
    layers = received.reshape(bricks, 4, row_cells, col_cells // bricks)
    result = layers[0]
    for brick in range(1, bricks):
        result = over_blend(result, layers[brick])
    return result


def solution(mesh):
    return jax.shard_map(
        shards,
        mesh=mesh,
        in_specs=(P("depth", "plane", None), P("depth", "plane", None), P(), P()),
        out_specs=P(None, "plane", "depth"),
        check_vma=False,
    )
```

profile of v0, /device:TPU:6, one launch (start us, length us, event | category | flops | bytes accessed | tf_op | source)
XLA Modules:
  0.0 121.5 jit_solution(16045488047696426419)
XLA Ops:
  0.0 0.8 fusion.45
  0.8 1.3 %collective-permute-start.1 = (bf16[2,8,1536]{2,1,0:T(8,128)(2,1)S(1)}, bf16[2,8,1536]{2,1,0:T(8,128)(2,1)S(1)}, u32[]{:S(2)}, u32[]{:S(2)}) collective-permute-start(bf16[2,8,1536]{2,1,0:T(8,128)(2,1)S(1)} %get-tuple-element.26), channel_id=1, source_target_pairs={{96,0},{192,96},{288,192},{384,288},{480,384},{576,480},{672,576},... | collective-permute-start | bytes 147464 | tf_op jit(solution)/shard_map/ppermute | solution.py:22
  2.1 4.5 %collective-permute-start = (bf16[2,8,1536]{2,1,0:T(8,128)(2,1)S(1)}, bf16[2,8,1536]{2,1,0:T(8,128)(2,1)S(1)}, u32[]{:S(2)}, u32[]{:S(2)}) collective-permute-start(bf16[2,8,1536]{2,1,0:T(8,128)(2,1)S(1)} %get-tuple-element.27), channel_id=1, source_target_pairs={{0,96},{96,192},{192,288},{288,384},{384,480},{480,576},{576,672},... | collective-permute-start | bytes 147464 | tf_op jit(solution)/shard_map/ppermute | solution.py:21
  6.7 2.1 %fusion.46 = (f32[1,1]{1,0:T(1,128)}, f32[1,1]{1,0:T(1,128)}, f32[1,1]{1,0:T(1,128)}, f32[1,1]{1,0:T(1,128)}, f32[1,1]{1,0:T(1,128)}, /*index=5*/f32[1,1]{1,0:T(...) fusion(f32[3,16]{1,0:T(4,128)} %param.6), kind=kLoop, calls=%fused_computation.114 | loop fusion | bytes 152 | tf_op jit(solution)/shard_map/slice | solution.py:65
  8.8 0.1 broadcast_and_fusion
  8.9 1.9 %fusion.49 = (f32[1]{0:T(128)}, f32[1]{0:T(128)}, f32[1]{0:T(128)}, f32[1]{0:T(128)}, f32[1]{0:T(128)}, /*index=5*/f32[1]{0:T(128)}, f32[1]{0:T(128)}, f32[1]{0:...) fusion(f32[16]{0:T(128)} %param.7), kind=kLoop, calls=%fused_computation.117 | loop fusion | bytes 128 | tf_op jit(solution)/shard_map/slice | solution.py:63
  10.8 0.0 collective-permute-done
  10.9 1.0 constant_dynamic-update-slice_fusion.1
  11.9 0.0 collective-permute-done.1
  11.9 0.2 fusion.44
  12.1 1.9 %collective-permute-start.2 = (bf16[20,2,1536]{2,1,0:T(2,128)(2,1)S(1)}, bf16[20,2,1536]{2,1,0:T(2,128)(2,1)S(1)}, u32[]{:S(2)}, u32[]{:S(2)}) collective-permute-start(bf16[20,2,1536]{2,1,0:T(2,128)(2,1)S(1)} %get-tuple-element.24), channel_id=1, source_target_pairs={{0,1},{1,2},{2,3},{3,4},{4,5},{5,6},{6,7},{7,8},{8,9},{9,10},{10,1... | collective-permute-start | bytes 368648 | tf_op jit(solution)/shard_map/ppermute | solution.py:21
  14.0 13.7 %collective-permute-start.3 = (bf16[20,2,1536]{2,1,0:T(2,128)(2,1)S(1)}, bf16[20,2,1536]{2,1,0:T(2,128)(2,1)S(1)}, u32[]{:S(2)}, u32[]{:S(2)}) collective-permute-start(bf16[20,2,1536]{2,1,0:T(2,128)(2,1)S(1)} %get-tuple-element.25), channel_id=1, source_target_pairs={{1,0},{2,1},{3,2},{4,3},{5,4},{6,5},{7,6},{8,7},{9,8},{10,9},{11,1... | collective-permute-start | bytes 368648 | tf_op jit(solution)/shard_map/ppermute | solution.py:22
  27.8 1.7 %fusion.48 = (f32[1,1]{1,0:T(1,128)}, f32[1,1]{1,0:T(1,128)}, f32[1,1]{1,0:T(1,128)}, f32[1,1]{1,0:T(1,128)}, f32[1,1]{1,0:T(1,128)}, /*index=5*/f32[1,1]{1,0:T(...) fusion(f32[3,16]{1,0:T(4,128)} %param.6), kind=kLoop, calls=%fused_computation.116 | loop fusion | bytes 80 | tf_op jit(solution)/shard_map/slice | solution.py:66
  29.5 2.1 %fusion.47 = (f32[1,1]{1,0:T(1,128)}, f32[1,1]{1,0:T(1,128)}, f32[1,1]{1,0:T(1,128)}, f32[1,1]{1,0:T(1,128)}, f32[1,1]{1,0:T(1,128)}, /*index=5*/f32[1,1]{1,0:T(...) fusion(f32[3,16]{1,0:T(4,128)} %param.6), kind=kLoop, calls=%fused_computation.115 | loop fusion | bytes 152 | tf_op jit(solution)/shard_map/slice | solution.py:65
  31.6 0.0 collective-permute-done.2
  31.6 0.0 collective-permute-done.3
  31.6 0.4 maximum_convert_fusion
  32.1 0.3 fusion.5
  32.3 0.5 broadcast_multiply_fusion
  32.8 1.1 fusion.3
  33.9 0.2 broadcast_multiply_fusion.2
  34.1 0.3 broadcast_multiply_fusion.1
  34.4 0.2 fusion.16
  34.6 0.9 fusion.9
  35.5 0.0 copy-start
  35.5 0.5 fusion.13
  36.1 0.6 copy-done
  36.7 12.8 %fusion.20 = (f32[16,8,1536]{2,1,0:T(8,128)S(1)}, pred[16,8,1536]{2,1,0:T(8,128)(4,1)S(1)}, pred[16,8,1536]{2,1,0:T(8,128)(4,1)S(1)}, pred[16,8,1536]{2,1,0:T(8,...) fusion(f32[18,10,1536]{2,1,0:T(8,128)S(1)} %fusion.3, ...), kind=kLoop, calls=%fused_computation.43 | loop fusion | flops 7077888 | bytes 5505088 | tf_op jit(solution)/shard_map/mul | solution.py:67
  49.5 7.5 %fusion.50 = f32[16,8,1536]{2,1,0:T(8,128)S(1)} fusion(f32[16,8,1536]{2,1,0:T(8,128)S(1)} %get-tuple-element.7), kind=kOutput, calls=%fused_computation.118 | output fusion | flops 2949120 | bytes 1572864 | tf_op jit(solution)/shard_map/jit(cumsum)/reduce_window_sum | solution.py:68
  57.1 12.0 %multiply_reduce_fusion.2 = (f32[8,1536]{1,0:T(8,128)S(1)}, f32[16,8,1536]{2,1,0:T(8,128)S(1)}) fusion(pred[16,8,1536]{2,1,0:T(8,128)(4,1)S(1)} %get-tuple-element.23, pred[16,8,1536]{2,1,0:T(8,128)(4,1)S(1)} %get-tuple-element.22, pred[16,8,1536]{2,1,0:T(8,128)(4,1)S(1)} %get-tuple-element.21, pred[16,8,1536]{2,1,0:T(8,128)(4,1)S(1)} %get-tuple-element.20, ...), kind=kLoop, calls=%fused_computation.46 | loop fusion | flops 8835072 | bytes 9486400 | tf_op jit(solution)/shard_map/reduce_sum | solution.py:73
  69.1 11.2 %multiply_reduce_fusion.1 = f32[8,1536]{1,0:T(8,128)S(1)} fusion(f32[16,8,1536]{2,1,0:T(8,128)S(1)} %get-tuple-element.6, pred[16,8,1536]{2,1,0:T(8,128)(4,1)S(1)} %get-tuple-element.23, pred[16,8,1536]{2,1,0:T(8,128)(4,1)S(1)} %get-tuple-element.22, pred[16,8,1536]{2,1,0:T(8,128)(4,1)S(1)} %get-tuple-element.21, ...), kind=kLoop, calls=%fused_computation.45 | loop fusion | flops 3526656 | bytes 3981376 | tf_op jit(solution)/shard_map/reduce_sum | solution.py:74
  80.2 11.4 %multiply_reduce_fusion = f32[8,1536]{1,0:T(8,128)S(1)} fusion(f32[16,8,1536]{2,1,0:T(8,128)S(1)} %get-tuple-element.6, pred[16,8,1536]{2,1,0:T(8,128)(4,1)S(1)} %get-tuple-element.23, pred[16,8,1536]{2,1,0:T(8,128)(4,1)S(1)} %get-tuple-element.22, pred[16,8,1536]{2,1,0:T(8,128)(4,1)S(1)} %get-tuple-element.21, ...), kind=kLoop, calls=%fused_computation.44 | loop fusion | flops 3526656 | bytes 3981376 | tf_op jit(solution)/shard_map/reduce_sum | solution.py:75
  91.7 1.2 %copy.6 = f32[4,8,1536]{1,0,2:T(4,128)S(1)} copy(f32[4,8,1536]{2,1,0:T(8,128)S(1)} %pad_maximum_fusion) | data formatting | bytes 393216 | tf_op jit(solution)/shard_map/stack | solution.py:71
  92.9 3.6 %reshape.62 = f32[8,1,6144]{2,1,0:T(1,128)S(1)} reshape(f32[1536,4,8]{2,1,0:T(4,128)S(1)} %bitcast.136) | data formatting | bytes 393216
  96.5 16.7 %all_to_all.15 = f32[8,1,6144]{2,1,0:T(1,128)S(1)} all-to-all(f32[8,1,6144]{2,1,0:T(1,128)S(1)} %reshape.62), channel_id=1, replica_groups=mesh['depth'=8,'plane'=96] {'depth'}, dimensions={0} | all-to-all | bytes 393216 | tf_op jit(solution)/shard_map/all_to_all | solution.py:101
  113.2 0.5 broadcast.185
  113.7 1.1 reduce
  114.8 3.7 %reshape.63 = f32[1536,4,8]{2,1,0:T(4,128)S(1)} reshape(f32[8,6144]{1,0:T(8,128)S(1)} %reduce) | data formatting | bytes 393216
  118.6 2.1 %copy.7 = f32[4,8,8,192]{3,1,0,2:T(8,128)S(1)} copy(f32[4,8,8,192]{1,0,3,2:T(4,128)S(1)} %bitcast.137) | data formatting | bytes 393216 | tf_op jit(solution)/shard_map/all_to_all | solution.py:101
  120.9 0.6 fusion.24
  (19 shorter events, 0.2 us)
Async XLA Ops:
  0.8 11.1 %collective-permute-start.1 = (bf16[2,8,1536]{2,1,0:T(8,128)(2,1)S(1)}, bf16[2,8,1536]{2,1,0:T(8,128)(2,1)S(1)}, u32[]{:S(2)}, u32[]{:S(2)}) collective-permute-start(bf16[2,8,1536]{2,1,0:T(8,128)(2,1)S(1)} %get-tuple-element.26), channel_id=1, source_target_pairs={{96,0},{192,96},{288,192},{384,288},{480,384},{576,480},{672,576},... | collective-permute-start | bytes 147464 | tf_op jit(solution)/shard_map/ppermute | solution.py:22
  2.1 8.7 %collective-permute-start = (bf16[2,8,1536]{2,1,0:T(8,128)(2,1)S(1)}, bf16[2,8,1536]{2,1,0:T(8,128)(2,1)S(1)}, u32[]{:S(2)}, u32[]{:S(2)}) collective-permute-start(bf16[2,8,1536]{2,1,0:T(8,128)(2,1)S(1)} %get-tuple-element.27), channel_id=1, source_target_pairs={{0,96},{96,192},{192,288},{288,384},{384,480},{480,576},{576,672},... | collective-permute-start | bytes 147464 | tf_op jit(solution)/shard_map/ppermute | solution.py:21
  12.1 19.5 %collective-permute-start.2 = (bf16[20,2,1536]{2,1,0:T(2,128)(2,1)S(1)}, bf16[20,2,1536]{2,1,0:T(2,128)(2,1)S(1)}, u32[]{:S(2)}, u32[]{:S(2)}) collective-permute-start(bf16[20,2,1536]{2,1,0:T(2,128)(2,1)S(1)} %get-tuple-element.24), channel_id=1, source_target_pairs={{0,1},{1,2},{2,3},{3,4},{4,5},{5,6},{6,7},{7,8},{8,9},{9,10},{10,1... | collective-permute-start | bytes 368648 | tf_op jit(solution)/shard_map/ppermute | solution.py:21
  14.0 17.6 %collective-permute-start.3 = (bf16[20,2,1536]{2,1,0:T(2,128)(2,1)S(1)}, bf16[20,2,1536]{2,1,0:T(2,128)(2,1)S(1)}, u32[]{:S(2)}, u32[]{:S(2)}) collective-permute-start(bf16[20,2,1536]{2,1,0:T(2,128)(2,1)S(1)} %get-tuple-element.25), channel_id=1, source_target_pairs={{1,0},{2,1},{3,2},{4,3},{5,4},{6,5},{7,6},{8,7},{9,8},{10,9},{11,1... | collective-permute-start | bytes 368648 | tf_op jit(solution)/shard_map/ppermute | solution.py:22
  35.5 1.1 copy-start
where the time goes:
time: 123 us; the launch traced here: 121 us
  other arithmetic  61.2 us (50%)
  local copies, waits for them, and re-layouts  21.7 us (18%)
  starting transfers between devices  21.5 us (17%)
  blocking collectives  16.7 us (14%)
    all_to_all x1, blocking collectives, shards(): lax.all_to_all(partial_image, 'depth', split_axis=2, concat_axis=0, tiled...  16.7 us
    ppermute x2, starting transfers between devices, with_halo(): after = lax.ppermute(initial, axis, down)  15 us
    mul x1, other arithmetic, render_brick(): optical = extinct * (smooth * smooth + 0.25) * scale  12.8 us
    reduce_sum x1, other arithmetic, render_brick(): jnp.sum(weight * reds, axis=0)  12 us
    reduce_sum x1, other arithmetic, render_brick(): jnp.sum(weight * blues, axis=0)  11.4 us
    reduce_sum x1, other arithmetic, render_brick(): jnp.sum(weight * greens, axis=0)  11.2 us
    unnamed x6, local copies, waits for them, and re-layouts  9 us
    another operation x1, other arithmetic, render_brick(): running = jnp.cumsum(optical, axis=0)  7.53 us
  transfers between devices with their start and end apart: 4, of which 0 were waited for; matrix products, arithmetic and copies ran while one was open for 7% of the time, Pallas kernels for 0%

commit v1 on v0

v1 whole, which is shorter than its diff:
```python
import functools

import jax
import jax.numpy as jnp
import numpy as np
from jax import lax
from jax.experimental import pallas as pl
from jax.experimental.pallas import tpu as pltpu
from jax.sharding import PartitionSpec as P

LIGHT_Z = 0.64
LIGHT_X = 0.48
LIGHT_Y = 0.6
LANES = 128
MESH = pl.DeviceIdType.MESH

TENT = np.array([0.0, 1.0, 2.0, 1.0, 0.0]) / 4.0
TENT_TENT = np.array([1.0, 4.0, 6.0, 4.0, 1.0]) / 16.0
SLOPE_TENT = np.array([-1.0, -2.0, 0.0, 2.0, 1.0]) / 8.0
RESULTS = (
    (TENT, TENT, 1.0 / 4.0),
    (SLOPE_TENT, TENT_TENT, 1.0 / 16.0),
    (TENT_TENT, SLOPE_TENT, 1.0 / 16.0),
    (TENT_TENT, TENT_TENT, 1.0 / 8.0),
)


def banded(taps, count, case):
    matrix = np.zeros((count, count + 4))
    for o in range(count):
        matrix[o, o : o + 5] = taps
    if case == 0:
        matrix[:, 2] -= matrix[:, 0]
        matrix[:, 0:2] = 0.0
    if case == 2:
        matrix[:, count + 1] -= matrix[:, count + 3]
        matrix[:, count + 2 : count + 4] = 0.0
    return matrix


def halo_rows(zs, xs):
    rows = [(z + 2, x + 2) for z in range(zs) for x in range(xs)]
    rows += [(z, x + 2) for z in (0, 1) for x in range(xs)]
    rows += [(zs + 2 + z, x + 2) for z in (0, 1) for x in range(xs)]
    rows += [(z + 2, x) for z in range(zs) for x in (0, 1)]
    rows += [(z + 2, xs + 2 + x) for z in range(zs) for x in (0, 1)]
    for z0 in (0, zs + 2):
        for x0 in (0, xs + 2):
            rows += [(z0 + z, x0 + x) for z in (0, 1) for x in (0, 1)]
            rows += [(-1, -1)] * 4
    return rows


def tables(zs, xs):
    rows = halo_rows(zs, xs)
    zi = np.array([r[0] for r in rows])
    xi = np.array([r[1] for r in rows])
    keep = (zi >= 0).astype(np.float64)
    zi, xi = np.maximum(zi, 0), np.maximum(xi, 0)
    ztab = np.stack(
        [
            np.concatenate([banded(z_taps, zs, case)[:, zi] for z_taps, _, _ in RESULTS])
            for case in range(3)
        ]
    )
    xtab = np.stack(
        [
            np.concatenate(
                [banded(x_taps, xs, case)[:, xi] * keep * scale for _, x_taps, scale in RESULTS]
            )
            for case in range(3)
        ]
    )
    return ztab.astype(np.float32), xtab.astype(np.float32)


def edge_picker(zs, xs):
    own = {(z, x): z * xs + x for z in range(zs) for x in range(xs)}
    wanted = [own[z, x] for z in range(zs) for x in (0, 1)]
    wanted += [own[z, x] for z in range(zs) for x in (xs - 2, xs - 1)]
    for z0 in (0, zs - 2):
        for x0 in (0, xs - 2):
            wanted += [own[z0 + z, x0 + x] for z in (0, 1) for x in (0, 1)]
            wanted += [-1] * 4
    picker = np.zeros((len(wanted), zs * xs), np.float32)
    for row, source in enumerate(wanted):
        if source >= 0:
            picker[row, source] = 1.0
    return picker


def frame_kernel(
    zs, xs, cols, bricks, planes,
    dens_hbm, mat_hbm, color_ref, ext_ref, ztab_hbm, xtab_hbm, pick_hbm,
    out_ref,
    field, mats, ztab, xtab, pick, edges, taps, filtered, looked, lut, send, recv,
    load_sem, halo_send, halo_recv, part_send, part_recv,
):
    own = zs * xs
    me_z = lax.axis_index("depth")
    me_x = lax.axis_index("plane")

    def move(src, dst, sem):
        return pltpu.make_async_copy(src, dst, load_sem.at[sem])

    z_case = jnp.where(me_z == 0, 0, jnp.where(me_z == bricks - 1, 2, 1))
    x_case = jnp.where(me_x == 0, 0, jnp.where(me_x == planes - 1, 2, 1))
    loads = [
        move(dens_hbm, field.at[0:own, pl.ds(LANES, cols)], 0),
        move(pick_hbm, pick, 1),
        move(mat_hbm, mats, 2),
        move(ztab_hbm.at[z_case], ztab, 3),
        move(xtab_hbm.at[x_case], xtab, 4),
    ]
    for load in loads:
        load.start()

    def device(dz, dx):
        return (lax.rem(me_z + dz + bricks, bricks), lax.rem(me_x + dx + planes, planes))

    sides = [(dz, dx) for dz in (-1, 0, 1) for dx in (-1, 0, 1) if (dz, dx) != (0, 0)]
    others = [(dz, 0) for dz in range(2, bricks - 1)]
    barrier = pltpu.get_barrier_semaphore()
    for dz, dx in sides + others:
        pl.semaphore_signal(barrier, inc=1, device_id=device(dz, dx), device_id_type=MESH)

    loads[0].wait()
    loads[1].wait()
    body = pl.ds(LANES, cols)
    edges[...] = jnp.dot(
        pick[...], field[0:own, body], preferred_element_type=jnp.float32
    ).astype(jnp.bfloat16)

    pl.semaphore_wait(barrier, len(sides + others))

    z_lo, z_hi = own, own + 2 * xs
    x_lo = own + 4 * xs
    x_hi = x_lo + 2 * zs
    corner = x_hi + 2 * zs
    face = {
        (-1, 0): (dens_hbm.at[0 : 2 * xs], z_hi, 2 * xs),
        (1, 0): (dens_hbm.at[own - 2 * xs : own], z_lo, 2 * xs),
        (0, -1): (edges.at[0 : 2 * zs], x_hi, 2 * zs),
        (0, 1): (edges.at[2 * zs : 4 * zs], x_lo, 2 * zs),
        (-1, -1): (edges.at[4 * zs : 4 * zs + 8], corner + 24, 8),
        (-1, 1): (edges.at[4 * zs + 8 : 4 * zs + 16], corner + 16, 8),
        (1, -1): (edges.at[4 * zs + 16 : 4 * zs + 24], corner + 8, 8),
        (1, 1): (edges.at[4 * zs + 24 : 4 * zs + 32], corner, 8),
    }
    halos = []
    for n, (dz, dx) in enumerate(sides):
        src, row, count = face[dz, dx]
        halos.append(
            pltpu.make_async_remote_copy(
                src_ref=src,
                dst_ref=field.at[row : row + count, body],
                send_sem=halo_send.at[n],
                recv_sem=halo_recv.at[n],
                device_id=device(dz, dx),
                device_id_type=MESH,
            )
        )
    for halo in halos:
        halo.start()

    loads[3].wait()
    loads[4].wait()
    for n in range(len(RESULTS)):
        zc = ztab[n * zs : (n + 1) * zs, :]
        xc = xtab[n * xs : (n + 1) * xs, :]
        block = zc[:, None, :] * xc[None, :, :]
        taps[n * own : (n + 1) * own, :] = block.reshape(own, zc.shape[1]).astype(jnp.bfloat16)

    total_z = zs * bricks
    levels = ext_ref.shape[1]
    lut[...] = jnp.zeros_like(lut)
    lut[0:8, 0:levels] = jnp.broadcast_to(ext_ref[...], (8, levels)) * (
        -2.0 / total_z * float(np.log2(np.e))
    )
    for c in range(3):
        lut[8 * c + 8 : 8 * c + 16, 0:levels] = jnp.broadcast_to(
            color_ref[c : c + 1, :], (8, levels)
        )
    loads[2].wait()

    def look(z, _):
        rows = pl.ds(pl.multiple_of(z * xs, 8), xs)
        for t in range(cols // LANES):
            tile = slice(t * LANES, (t + 1) * LANES)
            index = mats[rows, tile]
            for c in range(4):
                looked[c, rows, tile] = jnp.take_along_axis(
                    lut[8 * c : 8 * c + 8, :], index, axis=1
                )
        return 0

    lax.fori_loop(0, zs, look, 0)

    for halo in halos:
        halo.wait()

    wide = 2 * LANES
    lane_full = lax.broadcasted_iota(jnp.int32, (4 * own, LANES), 1)
    for t in range(cols // wide):
        at = slice(LANES + t * wide, LANES + (t + 1) * wide)
        filtered[:, at] = jnp.dot(taps[...], field[:, at], preferred_element_type=jnp.float32)
    first = filtered[:, LANES : 2 * LANES]
    filtered[:, 0:LANES] = jnp.where(lane_full == LANES - 2, -pltpu.roll(first, LANES - 2, 1), 0.0)
    final = filtered[:, cols : cols + LANES]
    filtered[:, cols + LANES : cols + 2 * LANES] = jnp.where(
        lane_full == 1, -pltpu.roll(final, 2, 1), 0.0
    )

    part = 2 * cols // bricks
    tiles = part // LANES
    span = part + 2 * LANES
    mid = slice(LANES, LANES + part)
    lane = lax.broadcasted_iota(jnp.int32, (xs, LANES), 1)
    low = lane < LANES // 2
    half = LANES // 2

    def partial(dest):
        return pltpu.make_async_remote_copy(
            src_ref=send.at[dest],
            dst_ref=recv.at[me_z],
            send_sem=part_send.at[dest],
            recv_sem=part_recv.at[me_z],
            device_id=(dest, me_x),
            device_id_type=MESH,
        )

    def phase(i, _):
        offset = jnp.where(i == 0, 2, jnp.where(i == 1, 1, jnp.where(i == 2, 3, 0)))
        pair = lax.rem(lax.div(me_z, 2) + offset, bricks // 2)
        start = pl.multiple_of(pair * part, LANES)

        def cells(z, carry):
            clear, red, green, blue = carry
            row = pl.multiple_of(z * xs, 8)

            def near(n):
                u = filtered[pl.ds(row + n * own, xs), pl.ds(start, span)]
                return u

            def shifted(u, by):
                return pltpu.roll(u, by % span, 1)[:, mid]

            u = near(0)
            smooth = shifted(u, 1) + shifted(u, -1) + 2.0 * u[:, mid]
            u = near(1)
            gz = (shifted(u, 2) + shifted(u, -2)) + 4.0 * (shifted(u, 1) + shifted(u, -1)) + 6.0 * u[:, mid]
            u = near(2)
            gx = (shifted(u, 2) + shifted(u, -2)) + 4.0 * (shifted(u, 1) + shifted(u, -1)) + 6.0 * u[:, mid]
            u = near(3)
            gy = (shifted(u, -2) - shifted(u, 2)) + 2.0 * (shifted(u, -1) - shifted(u, 1))
            lit = 0.35 + 0.65 * jnp.abs(LIGHT_Z * gz + LIGHT_X * gx + LIGHT_Y * gy) * lax.rsqrt(
                gz * gz + gx * gx + gy * gy + 1.0
            )
            here = (pl.ds(row, xs), pl.ds(start, part))
            passed = clear * jnp.exp2(looked[(0,) + here] * (smooth * smooth + 0.25))
            weight = (clear - passed) * lit
            return (
                passed,
                red + weight * looked[(1,) + here],
                green + weight * looked[(2,) + here],
                blue + weight * looked[(3,) + here],
            )

        def group(g, carry):
            for k in range(4):
                carry = cells(g * 4 + k, carry)
            return carry

        zero = jnp.zeros((xs, part), jnp.float32)
        clear, red, green, blue = lax.fori_loop(
            0, zs // 4, group, (zero + 1.0, zero, zero, zero)
        )
        fronts = [v[:, 0:LANES] for v in (red, green, blue, clear)]
        mids = [v[:, LANES : 2 * LANES] for v in (red, green, blue, clear)]
        backs = [v[:, 2 * LANES : 3 * LANES] for v in (red, green, blue, clear)]
        swapped = [pltpu.roll(v, half, 1) for v in mids]
        even, odd = 2 * pair, 2 * pair + 1
        for c in range(4):
            send[even, c] = fronts[c]
            send[odd, c] = backs[c]
        for c in range(2):
            send[even, 4 + c] = jnp.where(low, mids[2 * c], swapped[2 * c + 1])
            send[odd, 4 + c] = jnp.where(low, swapped[2 * c], mids[2 * c + 1])
        for dest in (even, odd):

            @pl.when(dest != me_z)
            def _():
                partial(dest).start()

        return 0

    lax.fori_loop(0, bricks // 2, phase, 0)
    recv[me_z] = send[me_z]

    image = [jnp.zeros((xs, LANES), jnp.float32) for _ in range(5)]
    clear = jnp.ones((xs, LANES), jnp.float32)
    clear_half = clear
    for s in range(bricks):

        @pl.when(me_z != s)
        def _():
            pltpu.make_async_remote_copy(
                src_ref=send.at[s],
                dst_ref=recv.at[s],
                send_sem=part_send.at[s],
                recv_sem=part_recv.at[s],
                device_id=(s, me_x),
                device_id_type=MESH,
            ).wait()

        layer = [recv[s, c] for c in range(6)]
        for c in range(3):
            image[c] = image[c] + clear * layer[c]
        image[3] = image[3] + clear_half * layer[4]
        image[4] = image[4] + clear_half * layer[5]
        clear = clear * layer[3]
        clear_half = clear_half * jnp.where(low, pltpu.roll(layer[5], half, 1), layer[5])
    mains = image[0:3] + [1.0 - clear]
    tail = jnp.where(low, image[4], 1.0 - clear_half)
    halves = [image[3], pltpu.roll(image[3], half, 1), tail, pltpu.roll(tail, half, 1)]
    is_even = lax.rem(me_z, 2) == 0
    for c in range(4):
        turned = pltpu.roll(mains[c], half, 1)
        out_ref[c, :, 0:LANES] = jnp.where(is_even, mains[c], jnp.where(low, halves[c], turned))
        out_ref[c, :, LANES : LANES + half] = jnp.where(is_even, halves[c], turned)[:, 0:half]


def shards(density, material, tf_color, tf_extinction):
    bricks = lax.axis_size("depth")
    planes = lax.axis_size("plane")
    zs, xs, cols = density.shape
    own = zs * xs
    ztab, xtab = tables(zs, xs)
    picker = edge_picker(zs, xs)
    gathered = ztab.shape[2]
    hbm = pl.BlockSpec(memory_space=pl.ANY)
    vmem = pl.BlockSpec(memory_space=pltpu.VMEM)
    return pl.pallas_call(
        functools.partial(frame_kernel, zs, xs, cols, bricks, planes),
        out_shape=jax.ShapeDtypeStruct((4, xs, cols // bricks), jnp.float32),
        in_specs=[hbm, hbm, vmem, vmem, hbm, hbm, hbm],
        out_specs=vmem,
        scratch_shapes=[
            pltpu.VMEM((gathered, cols + 2 * LANES), jnp.bfloat16),
            pltpu.VMEM((own, cols), jnp.int32),
            pltpu.VMEM(ztab.shape[1:], jnp.float32),
            pltpu.VMEM(xtab.shape[1:], jnp.float32),
            pltpu.VMEM(picker.shape, jnp.bfloat16),
            pltpu.VMEM((picker.shape[0], cols), jnp.bfloat16),
            pltpu.VMEM((4 * own, gathered), jnp.bfloat16),
            pltpu.VMEM((4 * own, cols + 2 * LANES), jnp.float32),
            pltpu.VMEM((4, own, cols), jnp.float32),
            pltpu.VMEM((32, LANES), jnp.float32),
            pltpu.VMEM((bricks, 6, xs, LANES), jnp.float32),
            pltpu.VMEM((bricks, 6, xs, LANES), jnp.float32),
            pltpu.SemaphoreType.DMA((5,)),
            pltpu.SemaphoreType.DMA((8,)),
            pltpu.SemaphoreType.DMA((8,)),
            pltpu.SemaphoreType.DMA((bricks,)),
            pltpu.SemaphoreType.DMA((bricks,)),
        ],
        compiler_params=pltpu.CompilerParams(collective_id=0, has_side_effects=True),
        name="frame",
    )(
        density.reshape(own, cols),
        material.reshape(own, cols),
        tf_color,
        tf_extinction.reshape(1, -1),
        jnp.asarray(ztab),
        jnp.asarray(xtab),
        jnp.asarray(picker, jnp.bfloat16),
    )


def solution(mesh):
    return jax.shard_map(
        shards,
        mesh=mesh,
        in_specs=(P("depth", "plane", None), P("depth", "plane", None), P(), P()),
        out_specs=P(None, "plane", "depth"),
        check_vma=False,
    )
```

time: 123 us -> 35.7 us (0.29)
  the two profiles are of different devices: /device:TPU:6 before, /device:TPU:8 now
where the time goes in v1:
time: 35.7 us; the launch traced here: 35.5 us
  Pallas kernels  34.1 us (96%)
  local copies, waits for them, and re-layouts  1.38 us (4%)
    pallas_call x1, Pallas kernels, shards(): pl.pallas_call(functools.partial(frame_kernel, zs, xs, cols, bricks, plan...  34.1 us
    unnamed x1, local copies, waits for them, and re-layouts  1.38 us

profile of v1, /device:TPU:8, one launch (start us, length us, event | category | flops | bytes accessed | tf_op | source)
XLA Modules:
  0.0 35.5 jit_solution(13551303608568041472)
XLA Ops:
  0.0 34.1 %frame.1 = f32[4,8,192]{2,1,0:T(8,128)} custom-call(bf16[128,1536]{1,0:T(8,128)(2,1)} %bitcast.4, s32[128,1536]{1,0:T(8,128)} %bitcast.3, f32[3,16]{1,0:T(4,128)} %color_ref.1, f32[1,16]{1,0:T(1,128)} %bitcast.5, f32[3,64,256]{2,1,0:T(8,128)} %constant.6.clone.ztab_hbm, f32[3,32,256]{2,1,0:T(8,128)} %constant.7.clone.xtab_hbm, ...), custom_call_target="tpu_custom_call" | custom-call | tf_op jit(solution)/shard_map/frame/pallas_call | solution.py:343
  34.1 1.4 %copy.9 = f32[4,8,192]{2,1,0:T(8,128)} copy(f32[4,8,192]{2,1,0:T(8,128)} %frame.1) | data formatting | bytes 49152

commit v2 on v1

--- a/solution.py
+++ b/solution.py
@@ -18,11 +18,13 @@
 TENT_TENT = np.array([1.0, 4.0, 6.0, 4.0, 1.0]) / 16.0
 SLOPE_TENT = np.array([-1.0, -2.0, 0.0, 2.0, 1.0]) / 8.0
 RESULTS = (
-    (TENT, TENT, 1.0 / 4.0),
-    (SLOPE_TENT, TENT_TENT, 1.0 / 16.0),
-    (TENT_TENT, SLOPE_TENT, 1.0 / 16.0),
-    (TENT_TENT, TENT_TENT, 1.0 / 8.0),
+    (TENT, TENT, TENT),
+    (SLOPE_TENT, TENT_TENT, TENT_TENT),
+    (TENT_TENT, SLOPE_TENT, TENT_TENT),
+    (TENT_TENT, TENT_TENT, SLOPE_TENT),
 )
+SHIFTS = (0, -1, 1, -2, 2)
+USED = ((0, 3), (0, 5), (0, 5), (1, 5))
 
 
 def banded(taps, count, case):
@@ -38,7 +40,7 @@
     return matrix
 
 
-def halo_rows(zs, xs):
+def gathered_rows(zs, xs):
     rows = [(z + 2, x + 2) for z in range(zs) for x in range(xs)]
     rows += [(z, x + 2) for z in (0, 1) for x in range(xs)]
     rows += [(zs + 2 + z, x + 2) for z in (0, 1) for x in range(xs)]
@@ -52,26 +54,19 @@
 
 
 def tables(zs, xs):
-    rows = halo_rows(zs, xs)
+    rows = gathered_rows(zs, xs)
     zi = np.array([r[0] for r in rows])
     xi = np.array([r[1] for r in rows])
     keep = (zi >= 0).astype(np.float64)
     zi, xi = np.maximum(zi, 0), np.maximum(xi, 0)
-    ztab = np.stack(
-        [
-            np.concatenate([banded(z_taps, zs, case)[:, zi] for z_taps, _, _ in RESULTS])
-            for case in range(3)
-        ]
-    )
-    xtab = np.stack(
-        [
-            np.concatenate(
-                [banded(x_taps, xs, case)[:, xi] * keep * scale for _, x_taps, scale in RESULTS]
-            )
-            for case in range(3)
-        ]
-    )
-    return ztab.astype(np.float32), xtab.astype(np.float32)
+    along_z = [
+        np.concatenate([banded(taps[0], zs, case)[:, zi] for taps in RESULTS]) for case in range(3)
+    ]
+    along_x = [
+        np.concatenate([banded(taps[1], xs, case)[:, xi] * keep for taps in RESULTS])
+        for case in range(3)
+    ]
+    return np.stack(along_z).astype(np.float32), np.stack(along_x).astype(np.float32)
 
 
 def edge_picker(zs, xs):
@@ -91,97 +86,144 @@
 
 def frame_kernel(
     zs, xs, cols, bricks, planes,
-    dens_hbm, mat_hbm, color_ref, ext_ref, ztab_hbm, xtab_hbm, pick_hbm,
+    dens_hbm, mat_hbm, color_hbm, ext_hbm, ztab_hbm, xtab_hbm, pick_hbm,
     out_ref,
-    field, mats, ztab, xtab, pick, edges, taps, filtered, looked, lut, send, recv,
+    field, halo, mats, color, ext, ztab, xtab, pick, edges, corners, corners_in, taps, halo_taps,
+    filtered, looked, lut, send, recv,
     load_sem, halo_send, halo_recv, part_send, part_recv,
 ):
     own = zs * xs
     me_z = lax.axis_index("depth")
     me_x = lax.axis_index("plane")
 
-    def move(src, dst, sem):
-        return pltpu.make_async_copy(src, dst, load_sem.at[sem])
-
-    z_case = jnp.where(me_z == 0, 0, jnp.where(me_z == bricks - 1, 2, 1))
-    x_case = jnp.where(me_x == 0, 0, jnp.where(me_x == planes - 1, 2, 1))
-    loads = [
-        move(dens_hbm, field.at[0:own, pl.ds(LANES, cols)], 0),
-        move(pick_hbm, pick, 1),
-        move(mat_hbm, mats, 2),
-        move(ztab_hbm.at[z_case], ztab, 3),
-        move(xtab_hbm.at[x_case], xtab, 4),
-    ]
-    for load in loads:
-        load.start()
-
     def device(dz, dx):
         return (lax.rem(me_z + dz + bricks, bricks), lax.rem(me_x + dx + planes, planes))
 
-    sides = [(dz, dx) for dz in (-1, 0, 1) for dx in (-1, 0, 1) if (dz, dx) != (0, 0)]
+    sides = [(-1, -1), (-1, 1), (1, -1), (1, 1), (-1, 0), (1, 0), (0, -1), (0, 1)]
     others = [(dz, 0) for dz in range(2, bricks - 1)]
     barrier = pltpu.get_barrier_semaphore()
     for dz, dx in sides + others:
         pl.semaphore_signal(barrier, inc=1, device_id=device(dz, dx), device_id_type=MESH)
 
+    def move(src, dst, sem):
+        return pltpu.make_async_copy(src, dst, load_sem.at[sem])
+
+    z_case = jnp.where(me_z == 0, 0, jnp.where(me_z == bricks - 1, 2, 1))
+    x_case = jnp.where(me_x == 0, 0, jnp.where(me_x == planes - 1, 2, 1))
+    loads = [
+        move(dens_hbm, field.at[0:own], 0),
+        move(pick_hbm, pick, 1),
+        move(ztab_hbm.at[z_case], ztab, 2),
+        move(xtab_hbm.at[x_case], xtab, 3),
+        move(color_hbm, color, 4),
+        move(ext_hbm, ext, 5),
+        move(mat_hbm, mats, 6),
+    ]
+    for load in loads:
+        load.start()
+
     loads[0].wait()
     loads[1].wait()
-    body = pl.ds(LANES, cols)
-    edges[...] = jnp.dot(
-        pick[...], field[0:own, body], preferred_element_type=jnp.float32
+    picked = jnp.dot(
+        pick[...], field[0:own, :], preferred_element_type=jnp.float32
     ).astype(jnp.bfloat16)
+    edges[...] = picked[0 : 4 * zs]
+    for n in range(4):
+        corners[n] = picked[4 * zs + 8 * n : 4 * zs + 8 * n + 4]
 
     pl.semaphore_wait(barrier, len(sides + others))
 
-    z_lo, z_hi = own, own + 2 * xs
-    x_lo = own + 4 * xs
+    z_lo, z_hi = 0, 2 * xs
+    x_lo = 4 * xs
     x_hi = x_lo + 2 * zs
     corner = x_hi + 2 * zs
+    gathered = corner + 32
     face = {
-        (-1, 0): (dens_hbm.at[0 : 2 * xs], z_hi, 2 * xs),
-        (1, 0): (dens_hbm.at[own - 2 * xs : own], z_lo, 2 * xs),
-        (0, -1): (edges.at[0 : 2 * zs], x_hi, 2 * zs),
-        (0, 1): (edges.at[2 * zs : 4 * zs], x_lo, 2 * zs),
-        (-1, -1): (edges.at[4 * zs : 4 * zs + 8], corner + 24, 8),
-        (-1, 1): (edges.at[4 * zs + 8 : 4 * zs + 16], corner + 16, 8),
-        (1, -1): (edges.at[4 * zs + 16 : 4 * zs + 24], corner + 8, 8),
-        (1, 1): (edges.at[4 * zs + 24 : 4 * zs + 32], corner, 8),
+        (-1, 0): (dens_hbm.at[0 : 2 * xs], halo.at[z_hi : z_hi + 2 * xs]),
+        (1, 0): (dens_hbm.at[own - 2 * xs : own], halo.at[z_lo : z_lo + 2 * xs]),
+        (0, -1): (edges.at[0 : 2 * zs], halo.at[x_hi : x_hi + 2 * zs]),
+        (0, 1): (edges.at[2 * zs : 4 * zs], halo.at[x_lo : x_lo + 2 * zs]),
+        (-1, -1): (corners.at[0], corners_in.at[3]),
+        (-1, 1): (corners.at[1], corners_in.at[2]),
+        (1, -1): (corners.at[2], corners_in.at[1]),
+        (1, 1): (corners.at[3], corners_in.at[0]),
     }
     halos = []
     for n, (dz, dx) in enumerate(sides):
-        src, row, count = face[dz, dx]
+        src, dst = face[dz, dx]
         halos.append(
             pltpu.make_async_remote_copy(
                 src_ref=src,
-                dst_ref=field.at[row : row + count, body],
+                dst_ref=dst,
                 send_sem=halo_send.at[n],
                 recv_sem=halo_recv.at[n],
                 device_id=device(dz, dx),
                 device_id_type=MESH,
             )
         )
-    for halo in halos:
-        halo.start()
-
+    for transfer in halos:
+        transfer.start()
+
+    loads[2].wait()
     loads[3].wait()
-    loads[4].wait()
-    for n in range(len(RESULTS)):
+    for n, (_, _, y_taps) in enumerate(RESULTS):
         zc = ztab[n * zs : (n + 1) * zs, :]
         xc = xtab[n * xs : (n + 1) * xs, :]
-        block = zc[:, None, :] * xc[None, :, :]
-        taps[n * own : (n + 1) * own, :] = block.reshape(own, zc.shape[1]).astype(jnp.bfloat16)
+        block = (zc[:, None, :] * xc[None, :, :]).reshape(own, own + gathered)
+        rows = slice(n * own, (n + 1) * own)
+        for k in range(*USED[n]):
+            scaled = (block * float(y_taps[SHIFTS[k] + 2])).astype(jnp.bfloat16)
+            taps[rows, k * own : (k + 1) * own] = scaled[:, 0:own]
+            halo_taps[rows, k * gathered : (k + 1) * gathered] = scaled[:, own:]
+
+    def spread(ref, count):
+        for r in range(0, count, 16):
+            rows = ref[r : r + 16, :]
+            first, final = rows[:, 0:LANES], rows[:, cols - LANES : cols]
+            at = lax.broadcasted_iota(jnp.int32, first.shape, 1)
+            for k, shift in enumerate(SHIFTS):
+                if shift == 0:
+                    continue
+                to = slice(k * count + r, k * count + r + 16)
+                moved = pltpu.roll(rows, -shift % cols, 1)
+                ref[to, :] = moved
+                nothing = jnp.zeros_like(first)
+                if shift < 0:
+                    edge = jnp.where(at == -shift - 1, nothing, moved[:, 0:LANES])
+                    if shift == -2:
+                        edge = jnp.where(at == 0, -first, edge)
+                    ref[to, 0:LANES] = edge
+                else:
+                    edge = jnp.where(at == LANES - shift, nothing, moved[:, cols - LANES : cols])
+                    if shift == 2:
+                        edge = jnp.where(at == LANES - 1, -final, edge)
+                    ref[to, cols - LANES : cols] = edge
+
+    def contract(coefficients, ref, count, n, at):
+        lo, hi = USED[n]
+        return jnp.dot(
+            coefficients[n * own : (n + 1) * own, lo * count : hi * count],
+            ref[lo * count : hi * count, at],
+            preferred_element_type=jnp.float32,
+        )
+
+    wide = 2 * LANES
+    spread(field, own)
+    for t in range(cols // wide):
+        at = slice(t * wide, (t + 1) * wide)
+        for n in range(4):
+            filtered[n * own : (n + 1) * own, at] = contract(taps, field, own, n, at)
 
     total_z = zs * bricks
-    levels = ext_ref.shape[1]
+    for n in (4, 5, 6):
+        loads[n].wait()
+    levels = ext.shape[1]
     lut[...] = jnp.zeros_like(lut)
-    lut[0:8, 0:levels] = jnp.broadcast_to(ext_ref[...], (8, levels)) * (
+    lut[0:8, 0:levels] = jnp.broadcast_to(ext[...], (8, levels)) * (
         -2.0 / total_z * float(np.log2(np.e))
     )
     for c in range(3):
-        lut[8 * c + 8 : 8 * c + 16, 0:levels] = jnp.broadcast_to(
-            color_ref[c : c + 1, :], (8, levels)
-        )
-    loads[2].wait()
+        lut[8 * c + 8 : 8 * c + 16, 0:levels] = jnp.broadcast_to(color[c : c + 1, :], (8, levels))
 
     def look(z, _):
         rows = pl.ds(pl.multiple_of(z * xs, 8), xs)
@@ -196,25 +238,21 @@
 
     lax.fori_loop(0, zs, look, 0)
 
-    for halo in halos:
-        halo.wait()
-
-    wide = 2 * LANES
-    lane_full = lax.broadcasted_iota(jnp.int32, (4 * own, LANES), 1)
+    for transfer in halos:
+        transfer.wait()
+
+    for n in range(4):
+        halo[corner + 8 * n : corner + 8 * n + 8, :] = jnp.concatenate(
+            [corners_in[n], jnp.zeros_like(corners_in[n])], axis=0
+        )
+    spread(halo, gathered)
     for t in range(cols // wide):
-        at = slice(LANES + t * wide, LANES + (t + 1) * wide)
-        filtered[:, at] = jnp.dot(taps[...], field[:, at], preferred_element_type=jnp.float32)
-    first = filtered[:, LANES : 2 * LANES]
-    filtered[:, 0:LANES] = jnp.where(lane_full == LANES - 2, -pltpu.roll(first, LANES - 2, 1), 0.0)
-    final = filtered[:, cols : cols + LANES]
-    filtered[:, cols + LANES : cols + 2 * LANES] = jnp.where(
-        lane_full == 1, -pltpu.roll(final, 2, 1), 0.0
-    )
+        at = slice(t * wide, (t + 1) * wide)
+        for n in range(4):
+            rows = slice(n * own, (n + 1) * own)
+            filtered[rows, at] = filtered[rows, at] + contract(halo_taps, halo, gathered, n, at)
 
     part = 2 * cols // bricks
-    tiles = part // LANES
-    span = part + 2 * LANES
-    mid = slice(LANES, LANES + part)
     lane = lax.broadcasted_iota(jnp.int32, (xs, LANES), 1)
     low = lane < LANES // 2
     half = LANES // 2
@@ -238,25 +276,13 @@
             clear, red, green, blue = carry
             row = pl.multiple_of(z * xs, 8)
 
-            def near(n):
-                u = filtered[pl.ds(row + n * own, xs), pl.ds(start, span)]
-                return u
-
-            def shifted(u, by):
-                return pltpu.roll(u, by % span, 1)[:, mid]
-
-            u = near(0)
-            smooth = shifted(u, 1) + shifted(u, -1) + 2.0 * u[:, mid]
-            u = near(1)
-            gz = (shifted(u, 2) + shifted(u, -2)) + 4.0 * (shifted(u, 1) + shifted(u, -1)) + 6.0 * u[:, mid]
-            u = near(2)
-            gx = (shifted(u, 2) + shifted(u, -2)) + 4.0 * (shifted(u, 1) + shifted(u, -1)) + 6.0 * u[:, mid]
-            u = near(3)
-            gy = (shifted(u, -2) - shifted(u, 2)) + 2.0 * (shifted(u, -1) - shifted(u, 1))
+            here = (pl.ds(row, xs), pl.ds(start, part))
+            smooth, gz, gx, gy = [
+                filtered[pl.ds(row + n * own, xs), pl.ds(start, part)] for n in range(4)
+            ]
             lit = 0.35 + 0.65 * jnp.abs(LIGHT_Z * gz + LIGHT_X * gx + LIGHT_Y * gy) * lax.rsqrt(
                 gz * gz + gx * gx + gy * gy + 1.0
             )
-            here = (pl.ds(row, xs), pl.ds(start, part))
             passed = clear * jnp.exp2(looked[(0,) + here] * (smooth * smooth + 0.25))
             weight = (clear - passed) * lit
             return (
@@ -337,28 +363,35 @@
     own = zs * xs
     ztab, xtab = tables(zs, xs)
     picker = edge_picker(zs, xs)
-    gathered = ztab.shape[2]
+    gathered = ztab.shape[2] - own
     hbm = pl.BlockSpec(memory_space=pl.ANY)
     vmem = pl.BlockSpec(memory_space=pltpu.VMEM)
+    shifts = len(SHIFTS)
     return pl.pallas_call(
         functools.partial(frame_kernel, zs, xs, cols, bricks, planes),
         out_shape=jax.ShapeDtypeStruct((4, xs, cols // bricks), jnp.float32),
-        in_specs=[hbm, hbm, vmem, vmem, hbm, hbm, hbm],
+        in_specs=[hbm] * 7,
         out_specs=vmem,
         scratch_shapes=[
-            pltpu.VMEM((gathered, cols + 2 * LANES), jnp.bfloat16),
+            pltpu.VMEM((shifts * own, cols), jnp.bfloat16),
+            pltpu.VMEM((shifts * gathered, cols), jnp.bfloat16),
             pltpu.VMEM((own, cols), jnp.int32),
+            pltpu.VMEM(tf_color.shape, jnp.float32),
+            pltpu.VMEM((1, tf_extinction.shape[0]), jnp.float32),
             pltpu.VMEM(ztab.shape[1:], jnp.float32),
             pltpu.VMEM(xtab.shape[1:], jnp.float32),
             pltpu.VMEM(picker.shape, jnp.bfloat16),
-            pltpu.VMEM((picker.shape[0], cols), jnp.bfloat16),
-            pltpu.VMEM((4 * own, gathered), jnp.bfloat16),
-            pltpu.VMEM((4 * own, cols + 2 * LANES), jnp.float32),
+            pltpu.VMEM((4 * zs, cols), jnp.bfloat16),
+            pltpu.VMEM((4, 4, cols), jnp.bfloat16),
+            pltpu.VMEM((4, 4, cols), jnp.bfloat16),
+            pltpu.VMEM((4 * own, shifts * own), jnp.bfloat16),
+            pltpu.VMEM((4 * own, shifts * gathered), jnp.bfloat16),
+            pltpu.VMEM((4 * own, cols), jnp.float32),
             pltpu.VMEM((4, own, cols), jnp.float32),
             pltpu.VMEM((32, LANES), jnp.float32),
             pltpu.VMEM((bricks, 6, xs, LANES), jnp.float32),
             pltpu.VMEM((bricks, 6, xs, LANES), jnp.float32),
-            pltpu.SemaphoreType.DMA((5,)),
+            pltpu.SemaphoreType.DMA((7,)),
             pltpu.SemaphoreType.DMA((8,)),
             pltpu.SemaphoreType.DMA((8,)),
             pltpu.SemaphoreType.DMA((bricks,)),

time: 35.7 us -> 32.3 us (0.905)
  Pallas kernels: 34.1 us -> 30.7 us
    pallas_call x1, Pallas kernels: 34.1 us -> 30.7 us  [shards(): pl.pallas_call(functools.partial(frame_kernel, zs, xs, cols, bricks, plan...]
where the time goes in v2:
time: 32.3 us; the launch traced here: 32.1 us
  Pallas kernels  30.7 us (95%)
  local copies, waits for them, and re-layouts  1.38 us (4%)
    pallas_call x1, Pallas kernels, shards(): pl.pallas_call(functools.partial(frame_kernel, zs, xs, cols, bricks, plan...  30.7 us
    unnamed x1, local copies, waits for them, and re-layouts  1.38 us

profile of v2, /device:TPU:8, one launch (start us, length us, event | category | flops | bytes accessed | tf_op | source)
XLA Modules:
  0.0 32.1 jit_solution(3158098891541433127)
XLA Ops:
  0.0 30.7 %frame.1 = f32[4,8,192]{2,1,0:T(8,128)} custom-call(bf16[128,1536]{1,0:T(8,128)(2,1)} %bitcast.4, s32[128,1536]{1,0:T(8,128)} %bitcast.3, f32[3,16]{1,0:T(4,128)} %color_hbm.1, f32[1,16]{1,0:T(1,128)} %bitcast.5, f32[3,64,256]{2,1,0:T(8,128)} %constant.6.clone.ztab_hbm, f32[3,32,256]{2,1,0:T(8,128)} %constant.7.clone.xtab_hbm, ...), custom_call_target="tpu_custom_call" | custom-call | tf_op jit(solution)/shard_map/frame/pallas_call | solution.py:370
  30.8 1.4 %copy.9 = f32[4,8,192]{2,1,0:T(8,128)} copy(f32[4,8,192]{2,1,0:T(8,128)} %frame.1) | data formatting | bytes 49152

commit v3 on v2

--- a/solution.py
+++ b/solution.py
@@ -24,7 +24,6 @@
     (TENT_TENT, TENT_TENT, SLOPE_TENT),
 )
 SHIFTS = (0, -1, 1, -2, 2)
-USED = ((0, 3), (0, 5), (0, 5), (1, 5))
 
 
 def banded(taps, count, case):
@@ -89,7 +88,7 @@
     dens_hbm, mat_hbm, color_hbm, ext_hbm, ztab_hbm, xtab_hbm, pick_hbm,
     out_ref,
     field, halo, mats, color, ext, ztab, xtab, pick, edges, corners, corners_in, taps, halo_taps,
-    filtered, looked, lut, send, recv,
+    filtered, chunk, looked, lut, send, recv,
     load_sem, halo_send, halo_recv, part_send, part_recv,
 ):
     own = zs * xs
@@ -171,48 +170,40 @@
         xc = xtab[n * xs : (n + 1) * xs, :]
         block = (zc[:, None, :] * xc[None, :, :]).reshape(own, own + gathered)
         rows = slice(n * own, (n + 1) * own)
-        for k in range(*USED[n]):
+        for k in range(len(SHIFTS)):
             scaled = (block * float(y_taps[SHIFTS[k] + 2])).astype(jnp.bfloat16)
             taps[rows, k * own : (k + 1) * own] = scaled[:, 0:own]
             halo_taps[rows, k * gathered : (k + 1) * gathered] = scaled[:, own:]
 
-    def spread(ref, count):
+    def spread(ref, count, lo, hi):
+        left, right = max(lo - LANES, 0), min(hi + LANES, cols)
         for r in range(0, count, 16):
-            rows = ref[r : r + 16, :]
-            first, final = rows[:, 0:LANES], rows[:, cols - LANES : cols]
+            rows = ref[r : r + 16, left:right]
+            first, final = rows[:, 0:LANES], rows[:, right - left - LANES :]
+            nothing = jnp.zeros_like(first)
             at = lax.broadcasted_iota(jnp.int32, first.shape, 1)
             for k, shift in enumerate(SHIFTS):
                 if shift == 0:
                     continue
                 to = slice(k * count + r, k * count + r + 16)
-                moved = pltpu.roll(rows, -shift % cols, 1)
-                ref[to, :] = moved
-                nothing = jnp.zeros_like(first)
-                if shift < 0:
+                moved = pltpu.roll(rows, -shift % (right - left), 1)[:, lo - left : hi - left]
+                ref[to, lo:hi] = moved
+                if shift < 0 and lo == 0:
                     edge = jnp.where(at == -shift - 1, nothing, moved[:, 0:LANES])
                     if shift == -2:
                         edge = jnp.where(at == 0, -first, edge)
                     ref[to, 0:LANES] = edge
-                else:
-                    edge = jnp.where(at == LANES - shift, nothing, moved[:, cols - LANES : cols])
+                if shift > 0 and hi == cols:
+                    edge = jnp.where(at == LANES - shift, nothing, moved[:, hi - lo - LANES :])
                     if shift == 2:
                         edge = jnp.where(at == LANES - 1, -final, edge)
                     ref[to, cols - LANES : cols] = edge
 
-    def contract(coefficients, ref, count, n, at):
-        lo, hi = USED[n]
-        return jnp.dot(
-            coefficients[n * own : (n + 1) * own, lo * count : hi * count],
-            ref[lo * count : hi * count, at],
-            preferred_element_type=jnp.float32,
-        )
-
     wide = 2 * LANES
-    spread(field, own)
+    spread(field, own, 0, cols)
     for t in range(cols // wide):
         at = slice(t * wide, (t + 1) * wide)
-        for n in range(4):
-            filtered[n * own : (n + 1) * own, at] = contract(taps, field, own, n, at)
+        filtered[:, at] = jnp.dot(taps[...], field[:, at], preferred_element_type=jnp.float32)
 
     total_z = zs * bricks
     for n in (4, 5, 6):
@@ -245,17 +236,19 @@
         halo[corner + 8 * n : corner + 8 * n + 8, :] = jnp.concatenate(
             [corners_in[n], jnp.zeros_like(corners_in[n])], axis=0
         )
-    spread(halo, gathered)
-    for t in range(cols // wide):
-        at = slice(t * wide, (t + 1) * wide)
-        for n in range(4):
-            rows = slice(n * own, (n + 1) * own)
-            filtered[rows, at] = filtered[rows, at] + contract(halo_taps, halo, gathered, n, at)
 
     part = 2 * cols // bricks
     lane = lax.broadcasted_iota(jnp.int32, (xs, LANES), 1)
     low = lane < LANES // 2
     half = LANES // 2
+
+    def encode(values):
+        roots = jnp.sqrt(jnp.clip(jnp.concatenate(values, axis=0), 0.0, 1.0))
+        return (jnp.round(roots * 65535.0) - 32768.0).astype(jnp.int32).astype(jnp.int16)
+
+    def decode(code):
+        roots = (code.astype(jnp.int32).astype(jnp.float32) + 32768.0) * (1.0 / 65535.0)
+        return roots * roots
 
     def partial(dest):
         return pltpu.make_async_remote_copy(
@@ -267,19 +260,30 @@
             device_id_type=MESH,
         )
 
-    def phase(i, _):
-        offset = jnp.where(i == 0, 2, jnp.where(i == 1, 1, jnp.where(i == 2, 3, 0)))
-        pair = lax.rem(lax.div(me_z, 2) + offset, bricks // 2)
-        start = pl.multiple_of(pair * part, LANES)
+    pairs = bricks // 2
+    mine = lax.div(me_z, 2)
+
+    def pair_at(i):
+        pair = 0
+        for q in range(pairs):
+            far = sorted(range(pairs), key=lambda p: (p != 0, -min((p - q) % pairs, (q - p) % pairs)))
+            for k, p in enumerate(far):
+                pair = jnp.where((mine == q) & (i == k), p, pair)
+        return pair
+
+    def render(pair):
+        start = pl.multiple_of(pair * part, LANES) if not isinstance(pair, int) else pair * part
+        at = pl.ds(start, part)
+        chunk[...] = filtered[:, at] + jnp.dot(
+            halo_taps[...], halo[:, at], preferred_element_type=jnp.float32
+        )
 
         def cells(z, carry):
             clear, red, green, blue = carry
             row = pl.multiple_of(z * xs, 8)
 
             here = (pl.ds(row, xs), pl.ds(start, part))
-            smooth, gz, gx, gy = [
-                filtered[pl.ds(row + n * own, xs), pl.ds(start, part)] for n in range(4)
-            ]
+            smooth, gz, gx, gy = [chunk[pl.ds(row + n * own, xs), :] for n in range(4)]
             lit = 0.35 + 0.65 * jnp.abs(LIGHT_Z * gz + LIGHT_X * gx + LIGHT_Y * gy) * lax.rsqrt(
                 gz * gz + gx * gx + gy * gy + 1.0
             )
@@ -301,17 +305,18 @@
         clear, red, green, blue = lax.fori_loop(
             0, zs // 4, group, (zero + 1.0, zero, zero, zero)
         )
-        fronts = [v[:, 0:LANES] for v in (red, green, blue, clear)]
-        mids = [v[:, LANES : 2 * LANES] for v in (red, green, blue, clear)]
-        backs = [v[:, 2 * LANES : 3 * LANES] for v in (red, green, blue, clear)]
+        result = (red, green, blue, 1.0 - clear)
+        fronts = [v[:, 0:LANES] for v in result]
+        mids = [v[:, LANES : 2 * LANES] for v in result]
+        backs = [v[:, 2 * LANES : 3 * LANES] for v in result]
         swapped = [pltpu.roll(v, half, 1) for v in mids]
         even, odd = 2 * pair, 2 * pair + 1
-        for c in range(4):
-            send[even, c] = fronts[c]
-            send[odd, c] = backs[c]
-        for c in range(2):
-            send[even, 4 + c] = jnp.where(low, mids[2 * c], swapped[2 * c + 1])
-            send[odd, 4 + c] = jnp.where(low, swapped[2 * c], mids[2 * c + 1])
+        send[even] = encode(
+            fronts + [jnp.where(low, mids[2 * c], swapped[2 * c + 1]) for c in (0, 1)]
+        )
+        send[odd] = encode(
+            backs + [jnp.where(low, swapped[2 * c], mids[2 * c + 1]) for c in (0, 1)]
+        )
         for dest in (even, odd):
 
             @pl.when(dest != me_z)
@@ -320,7 +325,10 @@
 
         return 0
 
-    lax.fori_loop(0, bricks // 2, phase, 0)
+    spread(halo, gathered, 0, part)
+    render(0)
+    spread(halo, gathered, part, cols)
+    lax.fori_loop(1, pairs, lambda i, _: render(pair_at(i)), 0)
     recv[me_z] = send[me_z]
 
     image = [jnp.zeros((xs, LANES), jnp.float32) for _ in range(5)]
@@ -339,13 +347,14 @@
                 device_id_type=MESH,
             ).wait()
 
-        layer = [recv[s, c] for c in range(6)]
+        values = decode(recv[s])
+        layer = [values[c * xs : (c + 1) * xs] for c in range(6)]
         for c in range(3):
             image[c] = image[c] + clear * layer[c]
         image[3] = image[3] + clear_half * layer[4]
         image[4] = image[4] + clear_half * layer[5]
-        clear = clear * layer[3]
-        clear_half = clear_half * jnp.where(low, pltpu.roll(layer[5], half, 1), layer[5])
+        clear = clear * (1.0 - layer[3])
+        clear_half = clear_half * (1.0 - jnp.where(low, pltpu.roll(layer[5], half, 1), layer[5]))
     mains = image[0:3] + [1.0 - clear]
     tail = jnp.where(low, image[4], 1.0 - clear_half)
     halves = [image[3], pltpu.roll(image[3], half, 1), tail, pltpu.roll(tail, half, 1)]
@@ -369,7 +378,7 @@
     shifts = len(SHIFTS)
     return pl.pallas_call(
         functools.partial(frame_kernel, zs, xs, cols, bricks, planes),
-        out_shape=jax.ShapeDtypeStruct((4, xs, cols // bricks), jnp.float32),
+        out_shape=pltpu.VMEM((4, xs, cols // bricks), jnp.float32),
         in_specs=[hbm] * 7,
         out_specs=vmem,
         scratch_shapes=[
@@ -387,10 +396,11 @@
             pltpu.VMEM((4 * own, shifts * own), jnp.bfloat16),
             pltpu.VMEM((4 * own, shifts * gathered), jnp.bfloat16),
             pltpu.VMEM((4 * own, cols), jnp.float32),
+            pltpu.VMEM((4 * own, 2 * cols // bricks), jnp.float32),
             pltpu.VMEM((4, own, cols), jnp.float32),
             pltpu.VMEM((32, LANES), jnp.float32),
-            pltpu.VMEM((bricks, 6, xs, LANES), jnp.float32),
-            pltpu.VMEM((bricks, 6, xs, LANES), jnp.float32),
+            pltpu.VMEM((bricks, 6 * xs, LANES), jnp.int16),
+            pltpu.VMEM((bricks, 6 * xs, LANES), jnp.int16),
             pltpu.SemaphoreType.DMA((7,)),
             pltpu.SemaphoreType.DMA((8,)),
             pltpu.SemaphoreType.DMA((8,)),

time: 32.3 us -> 30.9 us (0.957)
  the two profiles are of different devices: /device:TPU:8 before, /device:TPU:56 now
where the time goes in v3:
time: 30.9 us; the launch traced here: 30.8 us
  Pallas kernels  30.1 us (97%)
  local copies, waits for them, and re-layouts  0.62 us (2%)
    pallas_call x1, Pallas kernels, shards(): pl.pallas_call(functools.partial(frame_kernel, zs, xs, cols, bricks, plan...  30.1 us

profile of v3, /device:TPU:56, one launch (start us, length us, event | category | flops | bytes accessed | tf_op | source)
XLA Modules:
  0.0 30.8 jit_solution(3377551880776064847)
XLA Ops:
  0.0 30.1 %frame.1 = f32[4,8,192]{2,1,0:T(8,128)S(1)} custom-call(bf16[128,1536]{1,0:T(8,128)(2,1)} %bitcast.4, s32[128,1536]{1,0:T(8,128)} %bitcast.3, f32[3,16]{1,0:T(4,128)} %color_hbm.1, f32[1,16]{1,0:T(1,128)} %bitcast.5, f32[3,64,256]{2,1,0:T(8,128)} %constant.6.clone.ztab_hbm, f32[3,32,256]{2,1,0:T(8,128)} %constant.7.clone.xtab_hbm, ...), custom_call_target="tpu_custom_call" | custom-call | tf_op jit(solution)/shard_map/frame/pallas_call | solution.py:379
  30.1 0.6 %copy.9 = f32[4,8,192]{2,1,0:T(8,128)} copy(f32[4,8,192]{2,1,0:T(8,128)S(1)} %frame.1) | data formatting | bytes 49152

commit v4 on v3

--- a/solution.py
+++ b/solution.py
@@ -89,7 +89,7 @@
     out_ref,
     field, halo, mats, color, ext, ztab, xtab, pick, edges, corners, corners_in, taps, halo_taps,
     filtered, chunk, looked, lut, send, recv,
-    load_sem, halo_send, halo_recv, part_send, part_recv,
+    load_sem, ready, halo_send, halo_recv, part_send, part_recv,
 ):
     own = zs * xs
     me_z = lax.axis_index("depth")
@@ -99,9 +99,8 @@
         return (lax.rem(me_z + dz + bricks, bricks), lax.rem(me_x + dx + planes, planes))
 
     sides = [(-1, -1), (-1, 1), (1, -1), (1, 1), (-1, 0), (1, 0), (0, -1), (0, 1)]
-    others = [(dz, 0) for dz in range(2, bricks - 1)]
     barrier = pltpu.get_barrier_semaphore()
-    for dz, dx in sides + others:
+    for dz, dx in sides:
         pl.semaphore_signal(barrier, inc=1, device_id=device(dz, dx), device_id_type=MESH)
 
     def move(src, dst, sem):
@@ -130,51 +129,11 @@
     for n in range(4):
         corners[n] = picked[4 * zs + 8 * n : 4 * zs + 8 * n + 4]
 
-    pl.semaphore_wait(barrier, len(sides + others))
-
     z_lo, z_hi = 0, 2 * xs
     x_lo = 4 * xs
     x_hi = x_lo + 2 * zs
     corner = x_hi + 2 * zs
     gathered = corner + 32
-    face = {
-        (-1, 0): (dens_hbm.at[0 : 2 * xs], halo.at[z_hi : z_hi + 2 * xs]),
-        (1, 0): (dens_hbm.at[own - 2 * xs : own], halo.at[z_lo : z_lo + 2 * xs]),
-        (0, -1): (edges.at[0 : 2 * zs], halo.at[x_hi : x_hi + 2 * zs]),
-        (0, 1): (edges.at[2 * zs : 4 * zs], halo.at[x_lo : x_lo + 2 * zs]),
-        (-1, -1): (corners.at[0], corners_in.at[3]),
-        (-1, 1): (corners.at[1], corners_in.at[2]),
-        (1, -1): (corners.at[2], corners_in.at[1]),
-        (1, 1): (corners.at[3], corners_in.at[0]),
-    }
-    halos = []
-    for n, (dz, dx) in enumerate(sides):
-        src, dst = face[dz, dx]
-        halos.append(
-            pltpu.make_async_remote_copy(
-                src_ref=src,
-                dst_ref=dst,
-                send_sem=halo_send.at[n],
-                recv_sem=halo_recv.at[n],
-                device_id=device(dz, dx),
-                device_id_type=MESH,
-            )
-        )
-    for transfer in halos:
-        transfer.start()
-
-    loads[2].wait()
-    loads[3].wait()
-    for n, (_, _, y_taps) in enumerate(RESULTS):
-        zc = ztab[n * zs : (n + 1) * zs, :]
-        xc = xtab[n * xs : (n + 1) * xs, :]
-        block = (zc[:, None, :] * xc[None, :, :]).reshape(own, own + gathered)
-        rows = slice(n * own, (n + 1) * own)
-        for k in range(len(SHIFTS)):
-            scaled = (block * float(y_taps[SHIFTS[k] + 2])).astype(jnp.bfloat16)
-            taps[rows, k * own : (k + 1) * own] = scaled[:, 0:own]
-            halo_taps[rows, k * gathered : (k + 1) * gathered] = scaled[:, own:]
-
     def spread(ref, count, lo, hi):
         left, right = max(lo - LANES, 0), min(hi + LANES, cols)
         for r in range(0, count, 16):
@@ -199,35 +158,91 @@
                         edge = jnp.where(at == LANES - 1, -final, edge)
                     ref[to, cols - LANES : cols] = edge
 
-    wide = 2 * LANES
-    spread(field, own, 0, cols)
-    for t in range(cols // wide):
-        at = slice(t * wide, (t + 1) * wide)
-        filtered[:, at] = jnp.dot(taps[...], field[:, at], preferred_element_type=jnp.float32)
-
-    total_z = zs * bricks
-    for n in (4, 5, 6):
-        loads[n].wait()
-    levels = ext.shape[1]
-    lut[...] = jnp.zeros_like(lut)
-    lut[0:8, 0:levels] = jnp.broadcast_to(ext[...], (8, levels)) * (
-        -2.0 / total_z * float(np.log2(np.e))
-    )
-    for c in range(3):
-        lut[8 * c + 8 : 8 * c + 16, 0:levels] = jnp.broadcast_to(color[c : c + 1, :], (8, levels))
-
-    def look(z, _):
-        rows = pl.ds(pl.multiple_of(z * xs, 8), xs)
-        for t in range(cols // LANES):
-            tile = slice(t * LANES, (t + 1) * LANES)
-            index = mats[rows, tile]
-            for c in range(4):
-                looked[c, rows, tile] = jnp.take_along_axis(
-                    lut[8 * c : 8 * c + 8, :], index, axis=1
-                )
-        return 0
-
-    lax.fori_loop(0, zs, look, 0)
+    def local():
+        loads[2].wait()
+        loads[3].wait()
+        for n, (_, _, y_taps) in enumerate(RESULTS):
+            zc = ztab[n * zs : (n + 1) * zs, :]
+            xc = xtab[n * xs : (n + 1) * xs, :]
+            block = (zc[:, None, :] * xc[None, :, :]).reshape(own, own + gathered)
+            rows = slice(n * own, (n + 1) * own)
+            for k in range(len(SHIFTS)):
+                scaled = (block * float(y_taps[SHIFTS[k] + 2])).astype(jnp.bfloat16)
+                taps[rows, k * own : (k + 1) * own] = scaled[:, 0:own]
+                halo_taps[rows, k * gathered : (k + 1) * gathered] = scaled[:, own:]
+
+        wide = 2 * LANES
+        spread(field, own, 0, cols)
+        for t in range(cols // wide):
+            at = slice(t * wide, (t + 1) * wide)
+            filtered[:, at] = jnp.dot(taps[...], field[:, at], preferred_element_type=jnp.float32)
+
+        total_z = zs * bricks
+        for n in (4, 5, 6):
+            loads[n].wait()
+        levels = ext.shape[1]
+        lut[...] = jnp.zeros_like(lut)
+        lut[0:8, 0:levels] = jnp.broadcast_to(ext[...], (8, levels)) * (
+            -2.0 / total_z * float(np.log2(np.e))
+        )
+        for c in range(3):
+            lut[8 * c + 8 : 8 * c + 16, 0:levels] = jnp.broadcast_to(color[c : c + 1, :], (8, levels))
+
+        def look(z, _):
+            rows = pl.ds(pl.multiple_of(z * xs, 8), xs)
+            for t in range(cols // LANES):
+                tile = slice(t * LANES, (t + 1) * LANES)
+                index = mats[rows, tile]
+                for c in range(4):
+                    looked[c, rows, tile] = jnp.take_along_axis(
+                        lut[8 * c : 8 * c + 8, :], index, axis=1
+                    )
+            return 0
+
+        lax.fori_loop(0, zs, look, 0)
+
+    ahead = lax.rem(me_x, 24) < 2
+    pl.when(ahead)(local)
+
+    pl.semaphore_wait(barrier, len(sides))
+
+    face = {
+        (-1, 0): (dens_hbm.at[0 : 2 * xs], halo.at[z_hi : z_hi + 2 * xs]),
+        (1, 0): (dens_hbm.at[own - 2 * xs : own], halo.at[z_lo : z_lo + 2 * xs]),
+        (0, -1): (edges.at[0 : 2 * zs], halo.at[x_hi : x_hi + 2 * zs]),
+        (0, 1): (edges.at[2 * zs : 4 * zs], halo.at[x_lo : x_lo + 2 * zs]),
+        (-1, -1): (corners.at[0], corners_in.at[3]),
+        (-1, 1): (corners.at[1], corners_in.at[2]),
+        (1, -1): (corners.at[2], corners_in.at[1]),
+        (1, 1): (corners.at[3], corners_in.at[0]),
+    }
+    halos = []
+    for n, (dz, dx) in enumerate(sides):
+        src, dst = face[dz, dx]
+        halos.append(
+            pltpu.make_async_remote_copy(
+                src_ref=src,
+                dst_ref=dst,
+                send_sem=halo_send.at[n],
+                recv_sem=halo_recv.at[n],
+                device_id=device(dz, dx),
+                device_id_type=MESH,
+            )
+        )
+    for transfer in halos:
+        transfer.start()
+
+    rounds = bricks // 2 - 1
+
+    def announce(r):
+        for dz in (-1, 1):
+            pl.semaphore_signal(ready.at[r], inc=1, device_id=device(dz, 0), device_id_type=MESH)
+
+    announce(0)
+    pl.when(jnp.logical_not(ahead))(local)
+    for r in range(1, rounds):
+        pl.semaphore_wait(ready.at[r - 1], 2)
+        announce(r)
 
     for transfer in halos:
         transfer.wait()
@@ -326,6 +341,7 @@
         return 0
 
     spread(halo, gathered, 0, part)
+    pl.semaphore_wait(ready.at[rounds - 1], 2)
     render(0)
     spread(halo, gathered, part, cols)
     lax.fori_loop(1, pairs, lambda i, _: render(pair_at(i)), 0)
@@ -402,6 +418,7 @@
             pltpu.VMEM((bricks, 6 * xs, LANES), jnp.int16),
             pltpu.VMEM((bricks, 6 * xs, LANES), jnp.int16),
             pltpu.SemaphoreType.DMA((7,)),
+            pltpu.SemaphoreType.REGULAR((bricks // 2 - 1,)),
             pltpu.SemaphoreType.DMA((8,)),
             pltpu.SemaphoreType.DMA((8,)),
             pltpu.SemaphoreType.DMA((bricks,)),

time: 30.9 us -> 30.3 us (0.981)
  Pallas kernels: 30.1 us -> 29.5 us
    pallas_call x1, Pallas kernels: 30.1 us -> 29.5 us  [shards(): pl.pallas_call(functools.partial(frame_kernel, zs, xs, cols, bricks, plan...]
where the time goes in v4:
time: 30.3 us; the launch traced here: 30.1 us
  Pallas kernels  29.5 us (97%)
  local copies, waits for them, and re-layouts  0.62 us (2%)
    pallas_call x1, Pallas kernels, shards(): pl.pallas_call(functools.partial(frame_kernel, zs, xs, cols, bricks, plan...  29.5 us
    unnamed x1, local copies, waits for them, and re-layouts  0.62 us

profile of v4, /device:TPU:56, one launch (start us, length us, event | category | flops | bytes accessed | tf_op | source)
XLA Modules:
  0.0 30.1 jit_solution(8740819216505947284)
XLA Ops:
  0.0 29.5 %frame.1 = f32[4,8,192]{2,1,0:T(8,128)S(1)} custom-call(bf16[128,1536]{1,0:T(8,128)(2,1)} %bitcast.4, s32[128,1536]{1,0:T(8,128)} %bitcast.3, f32[3,16]{1,0:T(4,128)} %color_hbm.1, f32[1,16]{1,0:T(1,128)} %bitcast.5, f32[3,64,256]{2,1,0:T(8,128)} %constant.6.clone.ztab_hbm, f32[3,32,256]{2,1,0:T(8,128)} %constant.7.clone.xtab_hbm, ...), custom_call_target="tpu_custom_call" | custom-call | tf_op jit(solution)/shard_map/frame/pallas_call | solution.py:395
  29.5 0.6 %copy.9 = f32[4,8,192]{2,1,0:T(8,128)} copy(f32[4,8,192]{2,1,0:T(8,128)S(1)} %frame.1) | data formatting | bytes 49152

commit v5 on v4

--- a/solution.py
+++ b/solution.py
@@ -41,10 +41,10 @@
 
 def gathered_rows(zs, xs):
     rows = [(z + 2, x + 2) for z in range(zs) for x in range(xs)]
+    rows += [(z + 2, x) for z in range(zs) for x in (0, 1)]
+    rows += [(z + 2, xs + 2 + x) for z in range(zs) for x in (0, 1)]
     rows += [(z, x + 2) for z in (0, 1) for x in range(xs)]
     rows += [(zs + 2 + z, x + 2) for z in (0, 1) for x in range(xs)]
-    rows += [(z + 2, x) for z in range(zs) for x in (0, 1)]
-    rows += [(z + 2, xs + 2 + x) for z in range(zs) for x in (0, 1)]
     for z0 in (0, zs + 2):
         for x0 in (0, xs + 2):
             rows += [(z0 + z, x0 + x) for z in (0, 1) for x in (0, 1)]
@@ -87,7 +87,7 @@
     zs, xs, cols, bricks, planes,
     dens_hbm, mat_hbm, color_hbm, ext_hbm, ztab_hbm, xtab_hbm, pick_hbm,
     out_ref,
-    field, halo, mats, color, ext, ztab, xtab, pick, edges, corners, corners_in, taps, halo_taps,
+    field, halo_x, halo_z, mats, color, ext, ztab, xtab, pick, edges, corners, corners_in, taps, taps_x, taps_z,
     filtered, chunk, looked, lut, send, recv,
     load_sem, ready, halo_send, halo_recv, part_send, part_recv,
 ):
@@ -98,7 +98,7 @@
     def device(dz, dx):
         return (lax.rem(me_z + dz + bricks, bricks), lax.rem(me_x + dx + planes, planes))
 
-    sides = [(-1, -1), (-1, 1), (1, -1), (1, 1), (-1, 0), (1, 0), (0, -1), (0, 1)]
+    sides = [(0, -1), (0, 1), (-1, -1), (-1, 1), (1, -1), (1, 1), (-1, 0), (1, 0)]
     barrier = pltpu.get_barrier_semaphore()
     for dz, dx in sides:
         pl.semaphore_signal(barrier, inc=1, device_id=device(dz, dx), device_id_type=MESH)
@@ -129,11 +129,11 @@
     for n in range(4):
         corners[n] = picked[4 * zs + 8 * n : 4 * zs + 8 * n + 4]
 
-    z_lo, z_hi = 0, 2 * xs
-    x_lo = 4 * xs
-    x_hi = x_lo + 2 * zs
-    corner = x_hi + 2 * zs
+    x_lo, x_hi = 0, 2 * zs
+    z_lo, z_hi, corner = 0, 2 * xs, 4 * xs
+    beside = 4 * zs
     gathered = corner + 32
+
     def spread(ref, count, lo, hi):
         left, right = max(lo - LANES, 0), min(hi + LANES, cols)
         for r in range(0, count, 16):
@@ -164,12 +164,15 @@
         for n, (_, _, y_taps) in enumerate(RESULTS):
             zc = ztab[n * zs : (n + 1) * zs, :]
             xc = xtab[n * xs : (n + 1) * xs, :]
-            block = (zc[:, None, :] * xc[None, :, :]).reshape(own, own + gathered)
+            block = (zc[:, None, :] * xc[None, :, :]).reshape(own, own + beside + gathered)
             rows = slice(n * own, (n + 1) * own)
             for k in range(len(SHIFTS)):
                 scaled = (block * float(y_taps[SHIFTS[k] + 2])).astype(jnp.bfloat16)
                 taps[rows, k * own : (k + 1) * own] = scaled[:, 0:own]
-                halo_taps[rows, k * gathered : (k + 1) * gathered] = scaled[:, own:]
+                taps_x[rows, k * beside : (k + 1) * beside] = scaled[:, own : own + beside]
+                ends = slice(k * gathered, (k + 1) * gathered)
+                taps_z[n * 4 * xs : n * 4 * xs + 2 * xs, ends] = scaled[0 : 2 * xs, own + beside :]
+                taps_z[n * 4 * xs + 2 * xs : (n + 1) * 4 * xs, ends] = scaled[own - 2 * xs :, own + beside :]
 
         wide = 2 * LANES
         spread(field, own, 0, cols)
@@ -207,10 +210,10 @@
     pl.semaphore_wait(barrier, len(sides))
 
     face = {
-        (-1, 0): (dens_hbm.at[0 : 2 * xs], halo.at[z_hi : z_hi + 2 * xs]),
-        (1, 0): (dens_hbm.at[own - 2 * xs : own], halo.at[z_lo : z_lo + 2 * xs]),
-        (0, -1): (edges.at[0 : 2 * zs], halo.at[x_hi : x_hi + 2 * zs]),
-        (0, 1): (edges.at[2 * zs : 4 * zs], halo.at[x_lo : x_lo + 2 * zs]),
+        (-1, 0): (dens_hbm.at[0 : 2 * xs], halo_z.at[z_hi : z_hi + 2 * xs]),
+        (1, 0): (dens_hbm.at[own - 2 * xs : own], halo_z.at[z_lo : z_lo + 2 * xs]),
+        (0, -1): (edges.at[0 : 2 * zs], halo_x.at[x_hi : x_hi + 2 * zs]),
+        (0, 1): (edges.at[2 * zs : 4 * zs], halo_x.at[x_lo : x_lo + 2 * zs]),
         (-1, -1): (corners.at[0], corners_in.at[3]),
         (-1, 1): (corners.at[1], corners_in.at[2]),
         (1, -1): (corners.at[2], corners_in.at[1]),
@@ -244,11 +247,14 @@
         pl.semaphore_wait(ready.at[r - 1], 2)
         announce(r)
 
-    for transfer in halos:
-        transfer.wait()
+    for transfer in halos[0:2]:
+        transfer.wait_recv()
+    spread(halo_x, beside, 0, cols)
+    for transfer in halos[2:]:
+        transfer.wait_recv()
 
     for n in range(4):
-        halo[corner + 8 * n : corner + 8 * n + 8, :] = jnp.concatenate(
+        halo_z[corner + 8 * n : corner + 8 * n + 8, :] = jnp.concatenate(
             [corners_in[n], jnp.zeros_like(corners_in[n])], axis=0
         )
 
@@ -290,8 +296,14 @@
         start = pl.multiple_of(pair * part, LANES) if not isinstance(pair, int) else pair * part
         at = pl.ds(start, part)
         chunk[...] = filtered[:, at] + jnp.dot(
-            halo_taps[...], halo[:, at], preferred_element_type=jnp.float32
-        )
+            taps_x[...], halo_x[:, at], preferred_element_type=jnp.float32
+        )
+        ends = jnp.dot(taps_z[...], halo_z[:, at], preferred_element_type=jnp.float32)
+        for n in range(4):
+            for k, row in enumerate((n * own, (n + 1) * own - 2 * xs)):
+                from_row = (2 * n + k) * 2 * xs
+                rows = slice(row, row + 2 * xs)
+                chunk[rows, :] = chunk[rows, :] + ends[from_row : from_row + 2 * xs]
 
         def cells(z, carry):
             clear, red, green, blue = carry
@@ -340,12 +352,14 @@
 
         return 0
 
-    spread(halo, gathered, 0, part)
+    spread(halo_z, gathered, 0, part)
     pl.semaphore_wait(ready.at[rounds - 1], 2)
     render(0)
-    spread(halo, gathered, part, cols)
+    spread(halo_z, gathered, part, cols)
     lax.fori_loop(1, pairs, lambda i, _: render(pair_at(i)), 0)
     recv[me_z] = send[me_z]
+    for transfer in halos:
+        transfer.wait_send()
 
     image = [jnp.zeros((xs, LANES), jnp.float32) for _ in range(5)]
     clear = jnp.ones((xs, LANES), jnp.float32)
@@ -388,7 +402,7 @@
     own = zs * xs
     ztab, xtab = tables(zs, xs)
     picker = edge_picker(zs, xs)
-    gathered = ztab.shape[2] - own
+    gathered = ztab.shape[2] - own - 4 * zs
     hbm = pl.BlockSpec(memory_space=pl.ANY)
     vmem = pl.BlockSpec(memory_space=pltpu.VMEM)
     shifts = len(SHIFTS)
@@ -399,6 +413,7 @@
         out_specs=vmem,
         scratch_shapes=[
             pltpu.VMEM((shifts * own, cols), jnp.bfloat16),
+            pltpu.VMEM((shifts * 4 * zs, cols), jnp.bfloat16),
             pltpu.VMEM((shifts * gathered, cols), jnp.bfloat16),
             pltpu.VMEM((own, cols), jnp.int32),
             pltpu.VMEM(tf_color.shape, jnp.float32),
@@ -410,7 +425,8 @@
             pltpu.VMEM((4, 4, cols), jnp.bfloat16),
             pltpu.VMEM((4, 4, cols), jnp.bfloat16),
             pltpu.VMEM((4 * own, shifts * own), jnp.bfloat16),
-            pltpu.VMEM((4 * own, shifts * gathered), jnp.bfloat16),
+            pltpu.VMEM((4 * own, shifts * 4 * zs), jnp.bfloat16),
+            pltpu.VMEM((16 * xs, shifts * gathered), jnp.bfloat16),
             pltpu.VMEM((4 * own, cols), jnp.float32),
             pltpu.VMEM((4 * own, 2 * cols // bricks), jnp.float32),
             pltpu.VMEM((4, own, cols), jnp.float32),

time: 30.3 us -> 30 us (0.990)
  the two profiles are of different devices: /device:TPU:56 before, /device:TPU:8 now
where the time goes in v5:
time: 30 us; the launch traced here: 29.8 us
  Pallas kernels  29.2 us (97%)
  local copies, waits for them, and re-layouts  0.62 us (2%)
    pallas_call x1, Pallas kernels, shards(): pl.pallas_call(functools.partial(frame_kernel, zs, xs, cols, bricks, plan...  29.2 us
    unnamed x1, local copies, waits for them, and re-layouts  0.62 us

profile of v5, /device:TPU:8, one launch (start us, length us, event | category | flops | bytes accessed | tf_op | source)
XLA Modules:
  0.0 29.8 jit_solution(11014524470527822535)
XLA Ops:
  0.0 29.2 %frame.1 = f32[4,8,192]{2,1,0:T(8,128)S(1)} custom-call(bf16[128,1536]{1,0:T(8,128)(2,1)} %bitcast.4, s32[128,1536]{1,0:T(8,128)} %bitcast.3, f32[3,16]{1,0:T(4,128)} %color_hbm.1, f32[1,16]{1,0:T(1,128)} %bitcast.5, f32[3,64,256]{2,1,0:T(8,128)} %constant.6.clone.ztab_hbm, f32[3,32,256]{2,1,0:T(8,128)} %constant.7.clone.xtab_hbm, ...), custom_call_target="tpu_custom_call" | custom-call | tf_op jit(solution)/shard_map/frame/pallas_call | solution.py:409
  29.2 0.6 %copy.9 = f32[4,8,192]{2,1,0:T(8,128)} copy(f32[4,8,192]{2,1,0:T(8,128)S(1)} %frame.1) | data formatting | bytes 49152

commit v6 on v5

--- a/solution.py
+++ b/solution.py
@@ -99,10 +99,6 @@
         return (lax.rem(me_z + dz + bricks, bricks), lax.rem(me_x + dx + planes, planes))
 
     sides = [(0, -1), (0, 1), (-1, -1), (-1, 1), (1, -1), (1, 1), (-1, 0), (1, 0)]
-    barrier = pltpu.get_barrier_semaphore()
-    for dz, dx in sides:
-        pl.semaphore_signal(barrier, inc=1, device_id=device(dz, dx), device_id_type=MESH)
-
     def move(src, dst, sem):
         return pltpu.make_async_copy(src, dst, load_sem.at[sem])
 
@@ -117,7 +113,14 @@
         move(ext_hbm, ext, 5),
         move(mat_hbm, mats, 6),
     ]
-    for load in loads:
+    for load in loads[0:2]:
+        load.start()
+
+    barrier = pltpu.get_barrier_semaphore()
+    for dz, dx in sides:
+        pl.semaphore_signal(barrier, inc=1, device_id=device(dz, dx), device_id_type=MESH)
+
+    for load in loads[2:]:
         load.start()
 
     loads[0].wait()

time: 30 us -> 29.9 us (level)
  no operation moved by 1% of the time
where the time goes in v6:
time: 29.9 us; the launch traced here: 29.8 us
  Pallas kernels  29.1 us (97%)
  local copies, waits for them, and re-layouts  0.62 us (2%)
    pallas_call x1, Pallas kernels, shards(): pl.pallas_call(functools.partial(frame_kernel, zs, xs, cols, bricks, plan...  29.1 us
    unnamed x1, local copies, waits for them, and re-layouts  0.62 us

profile of v6, /device:TPU:8, one launch (start us, length us, event | category | flops | bytes accessed | tf_op | source)
XLA Modules:
  0.0 29.8 jit_solution(15953045100155006432)
XLA Ops:
  0.0 29.1 %frame.1 = f32[4,8,192]{2,1,0:T(8,128)S(1)} custom-call(bf16[128,1536]{1,0:T(8,128)(2,1)} %bitcast.4, s32[128,1536]{1,0:T(8,128)} %bitcast.3, f32[3,16]{1,0:T(4,128)} %color_hbm.1, f32[1,16]{1,0:T(1,128)} %bitcast.5, f32[3,64,256]{2,1,0:T(8,128)} %constant.6.clone.ztab_hbm, f32[3,32,256]{2,1,0:T(8,128)} %constant.7.clone.xtab_hbm, ...), custom_call_target="tpu_custom_call" | custom-call | tf_op jit(solution)/shard_map/frame/pallas_call | solution.py:412
  29.1 0.6 %copy.9 = f32[4,8,192]{2,1,0:T(8,128)} copy(f32[4,8,192]{2,1,0:T(8,128)S(1)} %frame.1) | data formatting | bytes 49152
